TPU v7x, 32 devices: a whole 2x2x4 slice. The times are simulated.
32 devices in a mesh: grp: 4 (over y, x), tp: 8 (over z, core).
Axes of the slice: x: 2, y: 2, z: 4, core: 2. Of those that a mesh axis runs over, the one named last changes fastest.
Arguments:
- teacher_in: bfloat16 [192, 8192], P('tp', 'grp'), may hold values from -6 to 6
- teacher_gate: bfloat16 [8192, 28672], P('grp', 'tp'), may hold values from -0.0625 to 0.0625
- teacher_up: bfloat16 [8192, 28672], P('grp', 'tp'), may hold values from -0.0625 to 0.0625
- teacher_down: bfloat16 [28672, 8192], P('tp', 'grp'), may hold values from -0.046875 to 0.046875
- student_in: bfloat16 [192, 4096], P('tp', 'grp'), may hold values from -6 to 6
- student_gate: bfloat16 [4096, 14336], P('grp', 'tp'), may hold values from -0.09375 to 0.09375
- student_up: bfloat16 [4096, 14336], P('grp', 'tp'), may hold values from -0.09375 to 0.09375
- student_down: bfloat16 [14336, 4096], P('tp', 'grp'), may hold values from -0.046875 to 0.046875
- projector: bfloat16 [4096, 4, 2048], P('grp', None, 'tp'), may hold values from -0.09375 to 0.09375
Outputs:
- grad_input: float32 [192, 4096], P('tp', 'grp')
- grad_gate: float32 [4096, 14336], P('grp', 'tp')
- grad_up: float32 [4096, 14336], P('grp', 'tp')
- grad_down: float32 [14336, 4096], P('tp', 'grp')
- grad_projector: float32 [4096, 4, 2048], P('grp', None, 'tp')
All inputs are finite; a program needn't handle non-finite values.
Results may differ from a plain program's by a relative error of at most 0.017.
Values may be sent and summed in bfloat16 or wider, within the bound.
No kernel may reach another device: no remote copies, remote signals or barrier semaphores. Data moves between devices by JAX's collectives and lax.ppermute only.
A program may use at most 192 MiB of HBM per device.

v0:
```python
import jax
import jax.numpy as jnp
from jax import lax
from jax.sharding import PartitionSpec as P


def body(
    teacher_in,
    teacher_gate,
    teacher_up,
    teacher_down,
    student_in,
    student_gate,
    student_up,
    student_down,
    projector,
):
    bf = jnp.bfloat16
    fl = jnp.float32
    teacher_pair = jnp.concatenate([teacher_gate, teacher_up], axis=1)
    teacher_width = teacher_gate.shape[1]
    teacher_partial = jnp.dot(
        lax.all_gather(teacher_in, "tp", axis=0, tiled=True),
        teacher_pair,
        preferred_element_type=fl,
    )
    teacher_pre = lax.psum_scatter(teacher_partial, "grp", scatter_dimension=0, tiled=True)
    teacher_hidden = (
        jax.nn.silu(teacher_pre[:, :teacher_width]) * teacher_pre[:, teacher_width:]
    ).astype(bf)
    teacher_sums = jnp.dot(
        lax.all_gather(teacher_hidden, "grp", axis=0, tiled=True),
        teacher_down,
        preferred_element_type=fl,
    )
    teacher_share = lax.psum_scatter(teacher_sums, "tp", scatter_dimension=1, tiled=True)
    teacher_feature = lax.all_to_all(
        teacher_share.astype(bf), "grp", split_axis=0, concat_axis=1, tiled=True
    )
    student_pair = jnp.concatenate([student_gate, student_up], axis=1)
    student_width = student_gate.shape[1]
    input_rows = lax.all_gather(student_in, "tp", axis=0, tiled=True)
    student_partial = jnp.dot(input_rows, student_pair, preferred_element_type=fl)
    student_pre = lax.psum_scatter(student_partial, "grp", scatter_dimension=0, tiled=True)
    gate_values = student_pre[:, :student_width]
    up_values = student_pre[:, student_width:]
    student_hidden = (jax.nn.silu(gate_values) * up_values).astype(bf)
    hidden_rows = lax.all_gather(student_hidden, "grp", axis=0, tiled=True)
    feature_sum = lax.psum(jnp.dot(hidden_rows, student_down, preferred_element_type=fl), "tp")
    student_feature = feature_sum.astype(bf)
    proj_matrix = projector.reshape(projector.shape[0], -1)
    projected = lax.psum_scatter(
        jnp.dot(student_feature, proj_matrix, preferred_element_type=fl),
        "grp",
        scatter_dimension=0,
        tiled=True,
    )
    residual_grad = (projected - teacher_feature.astype(fl)).astype(bf)
    residual_rows = lax.all_gather(residual_grad, "grp", axis=0, tiled=True)
    grad_projector = jnp.dot(student_feature.T, residual_rows, preferred_element_type=fl).reshape(
        projector.shape
    )
    feature_grad = lax.psum(
        jnp.dot(residual_rows, proj_matrix.T, preferred_element_type=fl), "tp"
    ).astype(bf)
    grad_down = jnp.dot(hidden_rows.T, feature_grad, preferred_element_type=fl)
    hidden_grad = lax.psum_scatter(
        jnp.dot(feature_grad, student_down.T, preferred_element_type=fl),
        "grp",
        scatter_dimension=0,
        tiled=True,
    )
    sigmoid_gate = jax.nn.sigmoid(gate_values)
    gate_grad = (
        hidden_grad * up_values * sigmoid_gate * (1.0 + gate_values * (1.0 - sigmoid_gate))
    ).astype(bf)
    up_grad = (hidden_grad * gate_values * sigmoid_gate).astype(bf)
    pair_rows = lax.all_gather(
        jnp.concatenate([gate_grad, up_grad], axis=1), "grp", axis=0, tiled=True
    )
    grad_pair = jnp.dot(input_rows.T, pair_rows, preferred_element_type=fl)
    grad_input = lax.psum_scatter(
        jnp.dot(pair_rows, student_pair.T, preferred_element_type=fl).astype(jnp.bfloat16),
        "tp",
        scatter_dimension=0,
        tiled=True,
    ).astype(jnp.float32)
    return (
        grad_input,
        grad_pair[:, :student_width],
        grad_pair[:, student_width:],
        grad_down,
        grad_projector,
    )


def solution(mesh):
    placed = (
        P("tp", "grp"),
        P("grp", "tp"),
        P("grp", "tp"),
        P("tp", "grp"),
        P("tp", "grp"),
        P("grp", "tp"),
        P("grp", "tp"),
        P("tp", "grp"),
        P("grp", None, "tp"),
    )
    return jax.shard_map(
        body,
        mesh=mesh,
        in_specs=placed,
        out_specs=(
            P("tp", "grp"),
            P("grp", "tp"),
            P("grp", "tp"),
            P("tp", "grp"),
            P("grp", None, "tp"),
        ),
        check_vma=False,
    )
```

profile of v0, /device:TPU:0, one launch (start us, length us, event | category | flops | bytes accessed | tf_op | source)
XLA Modules:
  0.0 422.7 jit_solution(930207206825908747)
XLA Ops:
  7.2 0.0 reduce-scatter.11.cloned.1.call-start
  7.2 17.4 %all_gather.20 = bf16[192,2048]{1,0:T(8,128)(2,1)S(1)} all-gather(bf16[24,2048]{1,0:T(8,128)(2,1)} %param.9), channel_id=1, replica_groups=mesh['grp'=4,'tp'=8] {'tp'}, dimensions={0}, use_global_device_ids=true | all-gather | bytes 884736 | tf_op jit(solution)/shard_map/all_gather | solution.py:23
  24.6 14.3 %fusion.4 = f32[192,7168]{1,0:T(8,128)} fusion(bf16[192,2048]{1,0:T(8,128)(2,1)S(1)} %all_gather.20, bf16[2048,3584]{1,0:T(8,128)(2,1)} %param.11, bf16[2048,3584]{1,0:T(8,128)(2,1)} %param.10), kind=kOutput, calls=%fused_computation.4 | convolution fusion | flops 5695864832 | bytes 35651584 | tf_op jit(solution)/shard_map/dot_general | solution.py:22
  39.0 0.0 all-gather.3.cloned.1.call-start
  39.0 64.8 %reduce-scatter.11.cloned.1.call-done = f32[48,7168]{1,0:T(8,128)} async-done(((f32[192,7168]{1,0:T(8,128)}), f32[48,7168]{1,0:T(8,128)}) %reduce-scatter.11.cloned.1.call-update) | async-done | bytes 1376272 | tf_op jit(solution)/shard_map/reduce_scatter | solution.py:27
  103.8 2.2 fusion.7
  106.0 0.0 reduce-scatter.7.cloned.1.call-start
  106.1 14.6 %all_gather.18 = bf16[192,1024]{1,0:T(8,128)(2,1)S(1)} all-gather(bf16[24,1024]{1,0:T(8,128)(2,1)S(1)} %copy-done.8), channel_id=1, replica_groups=mesh['grp'=4,'tp'=8] {'tp'}, dimensions={0}, use_global_device_ids=true | all-gather | bytes 442368 | tf_op jit(solution)/shard_map/all_gather | solution.py:42
  120.7 2.5 constant_dynamic-update-slice_fusion.1
  123.2 0.3 constant_dynamic-update-slice_fusion
  123.5 3.0 copy-done
  126.6 3.1 convolution_bitcast_fusion.1
  129.7 0.0 reduce-scatter.13.cloned.1.call-start
  129.8 5.7 %all-gather.3.cloned.1.call-done = bf16[192,3584]{1,0:T(8,128)(2,1)} async-done(((bf16[48,3584]{1,0:T(8,128)(2,1)}), bf16[192,3584]{1,0:T(8,128)(2,1)}) %all-gather.3.cloned.1.call-update) | async-done | bytes 1376272 | tf_op jit(solution)/shard_map/all_gather | solution.py:32
  135.4 9.8 %fusion.19 = f32[192,2048]{1,0:T(8,128)} fusion(bf16[192,3584]{1,0:T(8,128)(2,1)} %all-gather.3.cloned.1.call-done, bf16[3584,2048]{1,0:T(8,128)(2,1)} %param.12), kind=kOutput, calls=%fused_computation.30 | convolution fusion | flops 2818572288 | bytes 17629184 | tf_op jit(solution)/shard_map/dot_general | solution.py:31
  145.2 0.0 reduce-scatter.9.cloned.1.call-start
  145.3 2.2 copy.23
  147.4 32.3 %reduce-scatter.7.cloned.1.call-done = f32[48,3584]{1,0:T(8,128)} async-done(((f32[192,3584]{1,0:T(8,128)}), f32[48,3584]{1,0:T(8,128)}) %reduce-scatter.7.cloned.1.call-update) | async-done | bytes 688144 | tf_op jit(solution)/shard_map/reduce_scatter | solution.py:44
  179.7 1.2 multiply_convert_fusion.2
  180.9 10.7 %all_gather.19 = bf16[192,1792]{1,0:T(8,128)(2,1)S(1)} all-gather(bf16[48,1792]{1,0:T(8,128)(2,1)S(1)} %multiply_convert_fusion.2), channel_id=1, replica_groups=mesh['grp'=4,'tp'=8] {'grp'}, dimensions={0}, use_global_device_ids=true | all-gather | bytes 860160 | tf_op jit(solution)/shard_map/all_gather | solution.py:48
  191.6 3.8 fusion.18
  195.4 38.1 %all-reduce.2 = bf16[192,1024]{1,0:T(8,128)(2,1)S(1)} all-reduce(f32[192,1024]{1,0:T(8,128)} %fusion.18), channel_id=1, replica_groups=mesh['grp'=4,'tp'=8] {'tp'}, use_global_device_ids=true, to_apply=%region_1.2 | all-reduce | flops 196608 | bytes 1179648 | tf_op jit(solution)/shard_map/psum | solution.py:49
  233.5 1.5 fusion.24
  235.0 0.0 reduce-scatter.15.cloned.1.call-start
  235.1 0.9 convert_element_type.42
  236.1 7.8 %all_to_all.13 = bf16[4,48,256]{2,1,0:T(8,128)(2,1)S(1)} all-to-all(bf16[4,48,256]{2,1,0:T(8,128)(2,1)S(1)} %bitcast.40), channel_id=1, replica_groups=mesh['grp'=4,'tp'=8] {'grp'}, dimensions={0} | all-to-all | bytes 196608 | tf_op jit(solution)/shard_map/all_to_all | solution.py:37
  243.9 14.5 %reduce-scatter.9.cloned.1.call-done = f32[48,1024]{1,0:T(8,128)} async-done(((f32[192,1024]{1,0:T(8,128)}), f32[48,1024]{1,0:T(8,128)}) %reduce-scatter.9.cloned.1.call-update) | async-done | bytes 196624 | tf_op jit(solution)/shard_map/reduce_scatter | solution.py:52
  258.4 0.9 subtract_convert_fusion
  259.4 9.6 %all_gather.22 = bf16[192,1024]{1,0:T(8,128)(2,1)S(1)} all-gather(bf16[48,1024]{1,0:T(8,128)(2,1)S(1)} %subtract_convert_fusion), channel_id=1, replica_groups=mesh['grp'=4,'tp'=8] {'grp'}, dimensions={0}, use_global_device_ids=true | all-gather | bytes 491520 | tf_op jit(solution)/shard_map/all_gather | solution.py:59
  268.9 0.7 copy-done.4
  269.7 1.7 fusion.20
  271.4 35.0 %all-reduce.3 = bf16[192,1024]{1,0:T(8,128)(2,1)S(1)} all-reduce(f32[192,1024]{1,0:T(8,128)} %fusion.20), channel_id=1, replica_groups=mesh['grp'=4,'tp'=8] {'tp'}, use_global_device_ids=true, to_apply=%region_5.6 | all-reduce | flops 196608 | bytes 1179648 | tf_op jit(solution)/shard_map/psum | solution.py:63
  306.4 4.5 %fusion.22 = f32[192,1792]{1,0:T(8,128)} fusion(bf16[192,1024]{1,0:T(8,128)(2,1)S(1)} %all-reduce.3, bf16[1792,1024]{1,0:T(8,128)(2,1)} %param.16), kind=kOutput, calls=%fused_computation.33 | convolution fusion | flops 704643072 | bytes 5439488 | tf_op jit(solution)/shard_map/dot_general | solution.py:68
  310.9 0.2 all-gather.5.cloned.1.call-start
  311.1 27.0 %reduce-scatter.15.cloned.1.call-done = f32[48,1792]{1,0:T(8,128)} async-done(((f32[192,1792]{1,0:T(8,128)}), f32[48,1792]{1,0:T(8,128)}) %reduce-scatter.15.cloned.1.call-update) | async-done | bytes 344080 | tf_op jit(solution)/shard_map/reduce_scatter | solution.py:67
  338.2 1.1 multiply_convert_fusion.1
  339.3 0.7 pad_maximum_fusion
  340.1 0.0 reduce-scatter.17.cloned.1.call-start
  340.1 2.8 fusion.23
  342.9 5.3 %copy.21 = f32[1024,4,256]{2,1,0:T(4,128)} copy(f32[1024,4,256]{0,2,1:T(8,128)} %bitcast.35) | data formatting | bytes 8388608
  348.2 4.2 fusion.21
  352.4 17.1 %all-gather.5.cloned.1.call-done = bf16[192,3584]{1,0:T(8,128)(2,1)} async-done(((bf16[48,3584]{1,0:T(8,128)(2,1)}), bf16[192,3584]{1,0:T(8,128)(2,1)}) %all-gather.5.cloned.1.call-update) | async-done | bytes 1376272 | tf_op jit(solution)/shard_map/all_gather | solution.py:78
  369.4 6.9 %convolution_convert_fusion = bf16[192,1024]{1,0:T(8,128)(2,1)} fusion(bf16[192,3584]{1,0:T(8,128)(2,1)} %all-gather.5.cloned.1.call-done, bf16[1024,3584]{1,0:T(8,128)(2,1)} %copy-done), kind=kOutput, calls=%fused_computation.7 | convolution fusion | flops 1409482752 | bytes 9109504 | tf_op jit(solution)/shard_map/dot_general | solution.py:83
  376.4 7.3 %convolution_bitcast_fusion = f32[1024,3584]{0,1:T(8,128)} fusion(bf16[192,3584]{1,0:T(8,128)(2,1)S(1)} %copy-done.7, bf16[192,1024]{1,0:T(8,128)(2,1)S(1)} %copy-done.2), kind=kOutput, calls=%fused_computation.5 | convolution fusion | flops 1409286144 | bytes 16449536 | tf_op jit(solution)/shard_map/dot_general | solution.py:81
  383.7 13.9 %fusion.17 = (f32[1024,1792]{0,1:T(8,128)}, f32[1024,1792]{0,1:T(8,128)}) fusion(f32[1024,3584]{0,1:T(8,128)} %convolution_bitcast_fusion), kind=kLoop, calls=%fused_computation.28 | loop fusion | bytes 29360128 | tf_op jit(solution)/shard_map/slice | solution.py:91
  397.6 8.4 %copy.19 = f32[1024,1792]{1,0:T(8,128)} copy(f32[1024,1792]{0,1:T(8,128)} %get-tuple-element.16) | data formatting | bytes 14680064
  406.0 8.4 %copy.20 = f32[1024,1792]{1,0:T(8,128)} copy(f32[1024,1792]{0,1:T(8,128)} %get-tuple-element.15) | data formatting | bytes 14680064
  414.4 1.4 convert_element_type.51
  (28 shorter events, 0.2 us)
Async XLA Ops:
  7.2 96.6 %reduce-scatter.11.cloned.1.call-start = ((), (), s32[]{:S(2)}) async-start(), calls=%async_computation.9 | async-start | bytes 6881280 | tf_op jit(solution)/shard_map/reduce_scatter | solution.py:27
  38.9 67.1 %copy-start.8 = (bf16[24,1024]{1,0:T(8,128)(2,1)S(1)}, bf16[24,1024]{1,0:T(8,128)(2,1)}, u32[]{:S(2)}) copy-start(bf16[24,1024]{1,0:T(8,128)(2,1)} %param.13) | copy-start | bytes 147460
  39.0 96.5 %all-gather.3.cloned.1.call-start = ((), (), s32[]{:S(2)}) async-start(), calls=%async_computation.10 | async-start | bytes 1720320 | tf_op jit(solution)/shard_map/all_gather | solution.py:32
  106.0 73.7 %reduce-scatter.7.cloned.1.call-start = ((), (), s32[]{:S(2)}) async-start(), calls=%async_computation.7 | async-start | bytes 3440640 | tf_op jit(solution)/shard_map/reduce_scatter | solution.py:44
  106.1 17.1 %copy-start.3 = (bf16[1024,1792]{1,0:T(8,128)(2,1)S(1)}, bf16[1024,1792]{1,0:T(8,128)(2,1)}, u32[]{:S(2)}) copy-start(bf16[1024,1792]{1,0:T(8,128)(2,1)} %param.15) | copy-start | bytes 11010052
  120.7 2.8 copy-start.1
  123.5 3.1 copy-start
  129.7 105.4 %reduce-scatter.13.cloned.1.call-start = ((), (), s32[]{:S(2)}) async-start(), calls=%async_computation.11 | async-start | bytes 1769472 | tf_op jit(solution)/shard_map/reduce_scatter | solution.py:36
  145.2 113.2 %reduce-scatter.9.cloned.1.call-start = ((), (), s32[]{:S(2)}) async-start(), calls=%async_computation.8 | async-start | bytes 983040 | tf_op jit(solution)/shard_map/reduce_scatter | solution.py:52
  235.0 103.1 %reduce-scatter.15.cloned.1.call-start = ((), (), s32[]{:S(2)}) async-start(), calls=%async_computation.12 | async-start | bytes 1720320 | tf_op jit(solution)/shard_map/reduce_scatter | solution.py:67
  268.9 0.7 copy-start.4
  271.4 66.8 %copy-start.6 = (f32[48,3584]{1,0:T(8,128)S(1)}, f32[48,3584]{1,0:T(8,128)}, u32[]{:S(2)}) copy-start(f32[48,3584]{1,0:T(8,128)} %reduce-scatter.7.cloned.1.call-done) | copy-start | bytes 2064388
  271.4 68.7 %copy-start.5 = (bf16[192,1024]{1,0:T(8,128)(2,1)S(1)}, bf16[192,1024]{1,0:T(8,128)(2,1)}, u32[]{:S(2)}) copy-start(bf16[192,1024]{1,0:T(8,128)(2,1)} %copy-done.4) | copy-start | bytes 1179652
  310.9 58.5 %all-gather.5.cloned.1.call-start = ((), (), s32[]{:S(2)}) async-start(), calls=%async_computation.13 | async-start | bytes 1720320 | tf_op jit(solution)/shard_map/all_gather | solution.py:78
  340.1 74.3 %reduce-scatter.17.cloned.1.call-start = ((), (), s32[]{:S(2)}) async-start(), calls=%async_computation.14 | async-start | bytes 442368 | tf_op jit(solution)/shard_map/reduce_scatter | solution.py:82
  352.4 24.0 %copy-start.2 = (bf16[192,1024]{1,0:T(8,128)(2,1)S(1)}, bf16[192,1024]{1,0:T(8,128)(2,1)}, u32[]{:S(2)}) copy-start(bf16[192,1024]{1,0:T(8,128)(2,1)} %copy-done.1) | copy-start | bytes 1179652
  369.4 6.9 %copy-start.7 = (bf16[192,3584]{1,0:T(8,128)(2,1)S(1)}, bf16[192,3584]{1,0:T(8,128)(2,1)}, u32[]{:S(2)}) copy-start(bf16[192,3584]{1,0:T(8,128)(2,1)} %all-gather.5.cloned.1.call-done) | copy-start | bytes 4128772
Sparse Core Ops, SparseCore 0:
  39.1 64.6 reduce-scatter.10
  106.2 29.1 all-gather.2
  139.0 40.6 reduce-scatter.6
  182.4 36.0 reduce-scatter.12
  235.2 23.2 reduce-scatter.8
  311.0 27.0 reduce-scatter.14
  340.2 29.1 all-gather.4
  376.5 31.1 reduce-scatter.16
where the time goes:
time: 424 us; the launch traced here: 423 us
  waiting for transfers between devices  161 us (38%)
  blocking collectives  133 us (31%)
  matrix products  59.9 us (14%)
  local copies, waits for them, and re-layouts  44.7 us (11%)
  between operations  14.3 us (3%)
  other arithmetic  8.64 us (2%)
    reduce_scatter x1, waiting for transfers between devices, body(): lax.psum_scatter(teacher_partial, 'grp', scatter_dimension=0, tiled=True)  64.8 us
    psum x1, blocking collectives, body(): lax.psum(jnp.dot(hidden_rows, student_down, preferred_element_type=fl), '...  38.1 us
    psum x1, blocking collectives, body(): lax.psum(jnp.dot(residual_rows, proj_matrix.T, preferred_element_type=fl)...  35 us
    reduce_scatter x1, waiting for transfers between devices, body(): lax.psum_scatter(student_partial, 'grp', scatter_dimension=0, tiled=True)  32.3 us
    unnamed x23, local copies, waits for them, and re-layouts  30.4 us
    reduce_scatter x1, waiting for transfers between devices, body(): lax.psum_scatter(jnp.dot(feature_grad, student_down.T, preferred_element_...  27 us
    all_gather x1, blocking collectives, body(): lax.all_gather(teacher_in, 'tp', axis=0, tiled=True)  17.4 us
    all_gather x1, waiting for transfers between devices, body(): lax.all_gather(jnp.concatenate([gate_grad, up_grad], axis=1), 'grp', axis...  17.1 us
  transfers between devices with their start and end apart: 8, of which 6 were waited for; matrix products, arithmetic and copies ran while one was open for 18% of the time, Pallas kernels for 0%

commit v1 on v0

--- a/solution.py
+++ b/solution.py
@@ -46,7 +46,9 @@
     up_values = student_pre[:, student_width:]
     student_hidden = (jax.nn.silu(gate_values) * up_values).astype(bf)
     hidden_rows = lax.all_gather(student_hidden, "grp", axis=0, tiled=True)
-    feature_sum = lax.psum(jnp.dot(hidden_rows, student_down, preferred_element_type=fl), "tp")
+    feature_sum = jnp.sum(
+        lax.all_gather(jnp.dot(hidden_rows, student_down, preferred_element_type=fl), "tp"), axis=0
+    )
     student_feature = feature_sum.astype(bf)
     proj_matrix = projector.reshape(projector.shape[0], -1)
     projected = lax.psum_scatter(

time: 424 us -> 474 us (1.12)
  waiting for transfers between devices: 161 us -> 246 us
  blocking collectives: 133 us -> 96 us
    all_gather x0 -> x1, waiting for transfers between devices: none -> 54.6 us  [body(): lax.all_gather(jnp.dot(hidden_rows, student_down, preferred_element_type=...]
    psum x1 -> x0, blocking collectives: 38.1 us -> none  [body(): lax.psum(jnp.dot(hidden_rows, student_down, preferred_element_type=fl), '...]
    reduce_scatter x1, waiting for transfers between devices: 0.02 us -> 30.6 us  [body(): lax.psum_scatter(teacher_sums, 'tp', scatter_dimension=1, tiled=True)]
    reduce_scatter x1, waiting for transfers between devices: 64.8 us -> 40.4 us  [body(): lax.psum_scatter(teacher_partial, 'grp', scatter_dimension=0, tiled=True)]
    reduce_scatter x1, waiting for transfers between devices: 32.3 us -> 41.9 us  [body(): lax.psum_scatter(student_partial, 'grp', scatter_dimension=0, tiled=True)]
    all_gather x1, waiting for transfers between devices: 5.65 us -> 15.3 us  [body(): lax.all_gather(teacher_hidden, 'grp', axis=0, tiled=True)]
  transfers between devices with their start and end apart: 8 -> 9, of which waited for: 6 -> 8; matrix products, arithmetic and copies ran while one was open for 18% -> 17% of each run, Pallas kernels for 0% -> 0%
where the time goes in v1:
time: 474 us; the launch traced here: 473 us
  waiting for transfers between devices  246 us (52%)
  blocking collectives  96 us (20%)
  matrix products  59.8 us (13%)
  local copies, waits for them, and re-layouts  45.6 us (10%)
  between operations  14 us (3%)
  other arithmetic  12.1 us (3%)
    all_gather x1, waiting for transfers between devices, body(): lax.all_gather(jnp.dot(hidden_rows, student_down, preferred_element_type=...  54.6 us
    reduce_scatter x1, waiting for transfers between devices, body(): lax.psum_scatter(student_partial, 'grp', scatter_dimension=0, tiled=True)  41.9 us
    reduce_scatter x1, waiting for transfers between devices, body(): lax.psum_scatter(teacher_partial, 'grp', scatter_dimension=0, tiled=True)  40.4 us
    psum x1, blocking collectives, body(): lax.psum(jnp.dot(residual_rows, proj_matrix.T, preferred_element_type=fl)...  35.2 us
    unnamed x23, local copies, waits for them, and re-layouts  31.4 us
    reduce_scatter x1, waiting for transfers between devices, body(): lax.psum_scatter(teacher_sums, 'tp', scatter_dimension=1, tiled=True)  30.6 us
    reduce_scatter x1, waiting for transfers between devices, body(): lax.psum_scatter(jnp.dot(feature_grad, student_down.T, preferred_element_...  27.2 us
    reduce_scatter x1, waiting for transfers between devices, body(): lax.psum_scatter(jnp.dot(student_feature, proj_matrix, preferred_element_...  18.3 us
  transfers between devices with their start and end apart: 9, of which 8 were waited for; matrix products, arithmetic and copies ran while one was open for 17% of the time, Pallas kernels for 0%

profile of v1, /device:TPU:0, one launch (start us, length us, event | category | flops | bytes accessed | tf_op | source)
XLA Modules:
  0.0 473.4 jit_solution(17475646982938782250)
XLA Ops:
  7.2 17.4 %all_gather.28 = bf16[192,2048]{1,0:T(8,128)(2,1)S(1)} all-gather(bf16[24,2048]{1,0:T(8,128)(2,1)} %param.9), channel_id=1, replica_groups=mesh['grp'=4,'tp'=8] {'tp'}, dimensions={0}, use_global_device_ids=true | all-gather | bytes 884736 | tf_op jit(solution)/shard_map/all_gather | solution.py:23
  24.6 14.3 %fusion.4 = f32[192,7168]{1,0:T(8,128)} fusion(bf16[192,2048]{1,0:T(8,128)(2,1)S(1)} %all_gather.28, bf16[2048,3584]{1,0:T(8,128)(2,1)} %param.11, bf16[2048,3584]{1,0:T(8,128)(2,1)} %param.10), kind=kOutput, calls=%fused_computation.4 | convolution fusion | flops 5695864832 | bytes 35651584 | tf_op jit(solution)/shard_map/dot_general | solution.py:22
  39.0 0.0 reduce-scatter.7.cloned.1.call-start
  39.0 0.7 copy-done.8
  39.7 14.6 %all_gather.24 = bf16[192,1024]{1,0:T(8,128)(2,1)S(1)} all-gather(bf16[24,1024]{1,0:T(8,128)(2,1)S(1)} %copy-done.8), channel_id=1, replica_groups=mesh['grp'=4,'tp'=8] {'tp'}, dimensions={0}, use_global_device_ids=true | all-gather | bytes 442368 | tf_op jit(solution)/shard_map/all_gather | solution.py:42
  54.3 2.5 constant_dynamic-update-slice_fusion.1
  56.8 0.3 constant_dynamic-update-slice_fusion
  57.1 3.0 copy-done
  60.2 3.1 convolution_bitcast_fusion.1
  63.4 40.4 %reduce-scatter.11.cloned.1.call-done = f32[48,7168]{1,0:T(8,128)} async-done(((f32[192,7168]{1,0:T(8,128)}), f32[48,7168]{1,0:T(8,128)}) %reduce-scatter.11.cloned.1.call-update) | async-done | bytes 1376272 | tf_op jit(solution)/shard_map/reduce_scatter | solution.py:27
  103.8 2.2 fusion.7
  106.0 0.0 all-gather.9.cloned.1.call-start
  106.1 41.9 %reduce-scatter.7.cloned.1.call-done = f32[48,3584]{1,0:T(8,128)} async-done(((f32[192,3584]{1,0:T(8,128)}), f32[48,3584]{1,0:T(8,128)}) %reduce-scatter.7.cloned.1.call-update) | async-done | bytes 688144 | tf_op jit(solution)/shard_map/reduce_scatter | solution.py:44
  148.0 1.2 multiply_convert_fusion.2
  149.2 10.7 %all_gather.25 = bf16[192,1792]{1,0:T(8,128)(2,1)S(1)} all-gather(bf16[48,1792]{1,0:T(8,128)(2,1)S(1)} %multiply_convert_fusion.2), channel_id=1, replica_groups=mesh['grp'=4,'tp'=8] {'grp'}, dimensions={0}, use_global_device_ids=true | all-gather | bytes 860160 | tf_op jit(solution)/shard_map/all_gather | solution.py:48
  160.0 3.8 fusion.18
  163.8 15.3 %all-gather.5.cloned.1.call-done = bf16[192,3584]{1,0:T(8,128)(2,1)} async-done(((bf16[48,3584]{1,0:T(8,128)(2,1)}), bf16[192,3584]{1,0:T(8,128)(2,1)}) %all-gather.5.cloned.1.call-update) | async-done | bytes 1376272 | tf_op jit(solution)/shard_map/all_gather | solution.py:32
  179.1 9.8 %fusion.19 = f32[192,2048]{1,0:T(8,128)} fusion(bf16[192,3584]{1,0:T(8,128)(2,1)} %all-gather.5.cloned.1.call-done, bf16[3584,2048]{1,0:T(8,128)(2,1)} %param.12), kind=kOutput, calls=%fused_computation.30 | convolution fusion | flops 2818572288 | bytes 17629184 | tf_op jit(solution)/shard_map/dot_general | solution.py:31
  188.9 0.0 reduce-scatter.9.cloned.1.call-start
  188.9 2.3 copy.23
  191.3 54.6 %all-gather.9.cloned.1.call-done = f32[1536,1024]{1,0:T(8,128)} async-done(((f32[192,1024]{1,0:T(8,128)}), f32[1536,1024]{1,0:T(8,128)}) %all-gather.9.cloned.1.call-update) | async-done | bytes 6291472 | tf_op jit(solution)/shard_map/all_gather | solution.py:50
  245.9 3.5 reduce_sum.9
  249.4 1.5 fusion.24
  250.9 0.0 reduce-scatter.15.cloned.1.call-start
  250.9 30.6 %reduce-scatter.13.cloned.1.call-done = f32[192,256]{1,0:T(8,128)} async-done(((f32[192,2048]{1,0:T(8,128)}), f32[192,256]{1,0:T(8,128)}) %reduce-scatter.13.cloned.1.call-update) | async-done | bytes 196624 | tf_op jit(solution)/shard_map/reduce_scatter | solution.py:36
  281.5 0.9 convert_element_type.42
  282.5 8.5 %all_to_all.13 = bf16[4,48,256]{2,1,0:T(8,128)(2,1)S(1)} all-to-all(bf16[4,48,256]{2,1,0:T(8,128)(2,1)S(1)} %bitcast.42), channel_id=1, replica_groups=mesh['grp'=4,'tp'=8] {'grp'}, dimensions={0} | all-to-all | bytes 196608 | tf_op jit(solution)/shard_map/all_to_all | solution.py:37
  291.0 18.3 %reduce-scatter.9.cloned.1.call-done = f32[48,1024]{1,0:T(8,128)} async-done(((f32[192,1024]{1,0:T(8,128)}), f32[48,1024]{1,0:T(8,128)}) %reduce-scatter.9.cloned.1.call-update) | async-done | bytes 196624 | tf_op jit(solution)/shard_map/reduce_scatter | solution.py:54
  309.3 0.9 subtract_convert_fusion
  310.2 9.6 %all_gather.30 = bf16[192,1024]{1,0:T(8,128)(2,1)S(1)} all-gather(bf16[48,1024]{1,0:T(8,128)(2,1)S(1)} %subtract_convert_fusion), channel_id=1, replica_groups=mesh['grp'=4,'tp'=8] {'grp'}, dimensions={0}, use_global_device_ids=true | all-gather | bytes 491520 | tf_op jit(solution)/shard_map/all_gather | solution.py:61
  319.8 0.7 copy-done.4
  320.6 1.7 fusion.20
  322.3 35.2 %all-reduce.1 = bf16[192,1024]{1,0:T(8,128)(2,1)S(1)} all-reduce(f32[192,1024]{1,0:T(8,128)} %fusion.20), channel_id=1, replica_groups=mesh['grp'=4,'tp'=8] {'tp'}, use_global_device_ids=true, to_apply=%region_5.6 | all-reduce | flops 196608 | bytes 1179648 | tf_op jit(solution)/shard_map/psum | solution.py:65
  357.5 4.5 fusion.22
  362.0 0.0 all-gather.7.cloned.1.call-start
  362.0 27.2 %reduce-scatter.15.cloned.1.call-done = f32[48,1792]{1,0:T(8,128)} async-done(((f32[192,1792]{1,0:T(8,128)}), f32[48,1792]{1,0:T(8,128)}) %reduce-scatter.15.cloned.1.call-update) | async-done | bytes 344080 | tf_op jit(solution)/shard_map/reduce_scatter | solution.py:69
  389.2 1.1 multiply_convert_fusion.1
  390.4 0.8 pad_maximum_fusion
  391.2 2.8 fusion.23
  394.0 5.3 %copy.21 = f32[1024,4,256]{2,1,0:T(4,128)} copy(f32[1024,4,256]{0,2,1:T(8,128)} %bitcast.36) | data formatting | bytes 8388608
  399.2 4.2 fusion.21
  403.4 17.1 %all-gather.7.cloned.1.call-done = bf16[192,3584]{1,0:T(8,128)(2,1)} async-done(((bf16[48,3584]{1,0:T(8,128)(2,1)}), bf16[192,3584]{1,0:T(8,128)(2,1)}) %all-gather.7.cloned.1.call-update) | async-done | bytes 1376272 | tf_op jit(solution)/shard_map/all_gather | solution.py:80
  420.5 6.9 %convolution_convert_fusion = bf16[192,1024]{1,0:T(8,128)(2,1)} fusion(bf16[192,3584]{1,0:T(8,128)(2,1)} %all-gather.7.cloned.1.call-done, bf16[1024,3584]{1,0:T(8,128)(2,1)} %copy-done), kind=kOutput, calls=%fused_computation.7 | convolution fusion | flops 1409482752 | bytes 9109504 | tf_op jit(solution)/shard_map/dot_general | solution.py:85
  427.4 7.3 %convolution_bitcast_fusion = f32[1024,3584]{0,1:T(8,128)} fusion(bf16[192,3584]{1,0:T(8,128)(2,1)S(1)} %copy-done.7, bf16[192,1024]{1,0:T(8,128)(2,1)S(1)} %copy-done.2), kind=kOutput, calls=%fused_computation.5 | convolution fusion | flops 1409286144 | bytes 16449536 | tf_op jit(solution)/shard_map/dot_general | solution.py:83
  434.7 13.9 %fusion.17 = (f32[1024,1792]{0,1:T(8,128)}, f32[1024,1792]{0,1:T(8,128)}) fusion(f32[1024,3584]{0,1:T(8,128)} %convolution_bitcast_fusion), kind=kLoop, calls=%fused_computation.28 | loop fusion | bytes 29360128 | tf_op jit(solution)/shard_map/slice | solution.py:93
  448.7 8.4 %copy.19 = f32[1024,1792]{1,0:T(8,128)} copy(f32[1024,1792]{0,1:T(8,128)} %get-tuple-element.16) | data formatting | bytes 14680064
  457.0 8.4 %copy.20 = f32[1024,1792]{1,0:T(8,128)} copy(f32[1024,1792]{0,1:T(8,128)} %get-tuple-element.15) | data formatting | bytes 14680064
  465.4 1.4 convert_element_type.51
  (31 shorter events, 0.4 us)
Async XLA Ops:
  7.2 96.6 %reduce-scatter.11.cloned.1.call-start = ((), (), s32[]{:S(2)}) async-start(), calls=%async_computation.9 | async-start | bytes 6881280 | tf_op jit(solution)/shard_map/reduce_scatter | solution.py:27
  38.9 0.8 copy-start.8
  39.0 109.1 %reduce-scatter.7.cloned.1.call-start = ((), (), s32[]{:S(2)}) async-start(), calls=%async_computation.7 | async-start | bytes 3440640 | tf_op jit(solution)/shard_map/reduce_scatter | solution.py:44
  39.7 17.1 %copy-start.3 = (bf16[1024,1792]{1,0:T(8,128)(2,1)S(1)}, bf16[1024,1792]{1,0:T(8,128)(2,1)}, u32[]{:S(2)}) copy-start(bf16[1024,1792]{1,0:T(8,128)(2,1)} %param.15) | copy-start | bytes 11010052
  54.3 2.8 copy-start.1
  57.1 3.1 copy-start
  63.3 115.8 %all-gather.5.cloned.1.call-start = ((), (), s32[]{:S(2)}) async-start(), calls=%async_computation.10 | async-start | bytes 1720320 | tf_op jit(solution)/shard_map/all_gather | solution.py:32
  106.0 139.9 %all-gather.9.cloned.1.call-start = ((), (), s32[]{:S(2)}) async-start(), calls=%async_computation.15 | async-start | bytes 7077888 | tf_op jit(solution)/shard_map/all_gather | solution.py:50
  163.8 117.7 %reduce-scatter.13.cloned.1.call-start = ((), (), s32[]{:S(2)}) async-start(), calls=%async_computation.11 | async-start | bytes 1769472 | tf_op jit(solution)/shard_map/reduce_scatter | solution.py:36
  188.9 120.4 %reduce-scatter.9.cloned.1.call-start = ((), (), s32[]{:S(2)}) async-start(), calls=%async_computation.8 | async-start | bytes 983040 | tf_op jit(solution)/shard_map/reduce_scatter | solution.py:54
  250.9 138.3 %reduce-scatter.15.cloned.1.call-start = ((), (), s32[]{:S(2)}) async-start(), calls=%async_computation.12 | async-start | bytes 1720320 | tf_op jit(solution)/shard_map/reduce_scatter | solution.py:69
  319.8 0.7 copy-start.4
  322.3 66.9 %copy-start.6 = (f32[48,3584]{1,0:T(8,128)S(1)}, f32[48,3584]{1,0:T(8,128)}, u32[]{:S(2)}) copy-start(f32[48,3584]{1,0:T(8,128)} %reduce-scatter.7.cloned.1.call-done) | copy-start | bytes 2064388
  322.3 68.9 %copy-start.5 = (bf16[192,1024]{1,0:T(8,128)(2,1)S(1)}, bf16[192,1024]{1,0:T(8,128)(2,1)}, u32[]{:S(2)}) copy-start(bf16[192,1024]{1,0:T(8,128)(2,1)} %copy-done.4) | copy-start | bytes 1179652
  362.0 58.5 %all-gather.7.cloned.1.call-start = ((), (), s32[]{:S(2)}) async-start(), calls=%async_computation.13 | async-start | bytes 1720320 | tf_op jit(solution)/shard_map/all_gather | solution.py:80
  391.1 74.3 %reduce-scatter.17.cloned.1.call-start = ((), (), s32[]{:S(2)}) async-start(), calls=%async_computation.14 | async-start | bytes 442368 | tf_op jit(solution)/shard_map/reduce_scatter | solution.py:84
  403.4 24.0 %copy-start.2 = (bf16[192,1024]{1,0:T(8,128)(2,1)S(1)}, bf16[192,1024]{1,0:T(8,128)(2,1)}, u32[]{:S(2)}) copy-start(bf16[192,1024]{1,0:T(8,128)(2,1)} %copy-done.1) | copy-start | bytes 1179652
  420.5 6.9 %copy-start.7 = (bf16[192,3584]{1,0:T(8,128)(2,1)S(1)}, bf16[192,3584]{1,0:T(8,128)(2,1)}, u32[]{:S(2)}) copy-start(bf16[192,3584]{1,0:T(8,128)(2,1)} %all-gather.7.cloned.1.call-done) | copy-start | bytes 4128772
Sparse Core Ops, SparseCore 0:
  39.1 64.6 reduce-scatter.10
  107.4 40.6 reduce-scatter.6
  149.9 29.1 all-gather.4
  181.2 64.6 all-gather.8
  248.6 32.8 reduce-scatter.12
  284.8 24.3 reduce-scatter.8
  362.1 27.0 reduce-scatter.14
  391.3 29.1 all-gather.6
  427.5 31.0 reduce-scatter.16
